TPU v7x, 256 devices: a whole 4x4x8 slice. The times are simulated.
256 devices in a mesh: tok: 64 (over x, z, core), ch: 4 (over y).
Axes of the slice: x: 4, y: 4, z: 8, core: 2. Of those that a mesh axis runs over, the one named last changes fastest.
Arguments:
- inputs: float32 [65536, 1024], P('tok', 'ch'), may hold values from -6 to 6
- factor_one: float32 [512, 512], replicated, may hold values from -0.25 to 0.25
- twiddle: float32 [128, 512], P('tok'), may hold values from -4 to 4
- factor_two: float32 [128, 128], replicated, may hold values from -0.5 to 0.5
- w_up: bfloat16 [4, 256, 1024], P('ch', 'tok'), may hold values from -0.375 to 0.375
- w_down: bfloat16 [4, 1024, 256], P('ch', 'tok'), may hold values from -0.1875 to 0.1875
- out_cotangent: float32 [65536, 1024], P('tok', 'ch'), may hold values from -6 to 6
Outputs:
- outputs: float32 [65536, 1024], P('tok', 'ch')
- grad_inputs: float32 [65536, 1024], P('tok', 'ch')
- grad_factor_one: float32 [512, 512], replicated
- grad_factor_two: float32 [128, 128], replicated
- grad_up: float32 [4, 256, 1024], P('ch', 'tok')
- grad_down: float32 [4, 1024, 256], P('ch', 'tok')
All inputs are finite; a program needn't handle non-finite values.
Results may differ from a plain program's by a relative error of at most 0.0057.
Values may be sent and summed in bfloat16 or wider, within the bound.
A program may use at most 64 MiB of HBM per device.

v0:
```python
import math
import jax
import jax.numpy as jnp
from jax import lax
from jax.sharding import PartitionSpec as P

inv_root_two = 1.0 / math.sqrt(2.0)
inv_root_tau = 1.0 / math.sqrt(2.0 * math.pi)


def gelu_parts(value):
    cdf = 0.5 * (1.0 + jax.scipy.special.erf(value * inv_root_two))
    return (value * cdf, cdf + value * jnp.exp(-0.5 * value * value) * inv_root_tau)


def to_columns(block):
    count = lax.axis_size("tok")
    rows, width, chans = block.shape
    return lax.all_to_all(
        block.reshape(rows, count, width // count, chans),
        "tok",
        split_axis=1,
        concat_axis=0,
        tiled=True,
    ).reshape(count * rows, width // count, chans)


def to_rows(block):
    return lax.all_to_all(block, "tok", split_axis=0, concat_axis=1, tiled=True)


def local(inputs, factor_one, twiddle, factor_two, w_up, w_down, out_cotangent):
    high = lax.Precision.HIGHEST
    rows = twiddle.shape[0]
    width = twiddle.shape[1]
    chans = inputs.shape[1]
    panels = (
        lax.all_gather(w_up, "tok", axis=1, tiled=True),
        lax.all_gather(w_down, "tok", axis=1, tiled=True),
    )
    up_w = panels[0][0]
    down_w = panels[1][0]
    grid = inputs.reshape(rows, width, chans)
    first = jnp.einsum("kj,ijc->ikc", factor_one, grid, precision=high)
    mid = first * twiddle[:, :, None]
    mid_cols = to_columns(mid)
    mixed_cols = jnp.einsum("mi,ikc->mkc", factor_two, mid_cols, precision=high)
    mixed = to_rows(mixed_cols).reshape(rows * width, chans)
    gate = jax.nn.sigmoid(inputs)
    branch = inputs + gate * mixed
    normed = branch.astype(jnp.bfloat16)
    up = jnp.dot(normed, up_w, preferred_element_type=jnp.float32)
    active, slope = gelu_parts(up)
    hidden = active.astype(jnp.bfloat16)
    outputs = branch + jnp.dot(hidden, down_w, preferred_element_type=jnp.float32)
    cot = out_cotangent.astype(jnp.bfloat16)
    d_hidden = jnp.dot(cot, down_w.T, preferred_element_type=jnp.float32)
    d_up = (d_hidden * slope).astype(jnp.bfloat16)
    d_branch = out_cotangent + jnp.dot(d_up, up_w.T, preferred_element_type=jnp.float32)
    grad_down_part = jnp.dot(hidden.T, cot, preferred_element_type=jnp.float32)
    grad_up_part = jnp.dot(normed.T, d_up, preferred_element_type=jnp.float32)
    grad_up, grad_down = (
        lax.psum_scatter(grad_up_part[None], "tok", scatter_dimension=1, tiled=True),
        lax.psum_scatter(grad_down_part[None], "tok", scatter_dimension=1, tiled=True),
    )
    d_mixed = d_branch * gate
    direct = d_branch * (1.0 + gate * (1.0 - gate) * mixed)
    cot_cols = to_columns(d_mixed.reshape(rows, width, chans))
    d_mid_cols = jnp.einsum("mi,mkc->ikc", factor_two, cot_cols, precision=high)
    two_part = jnp.einsum("mkc,ikc->mi", cot_cols, mid_cols, precision=high)
    d_first = to_rows(d_mid_cols) * twiddle[:, :, None]
    one_part = jnp.einsum("ikc,ijc->kj", d_first, grid, precision=high)
    d_grid = jnp.einsum("kj,ikc->ijc", factor_one, d_first, precision=high)
    grad_inputs = direct + d_grid.reshape(rows * width, chans)
    grad_one, grad_two = lax.psum((one_part, two_part), ("tok", "ch"))
    return (outputs, grad_inputs, grad_one, grad_two, grad_up, grad_down)


def solution(mesh):
    in_specs = (
        P("tok", "ch"),
        P(),
        P("tok", None),
        P(),
        P("ch", "tok", None),
        P("ch", "tok", None),
        P("tok", "ch"),
    )
    out_specs = (
        P("tok", "ch"),
        P("tok", "ch"),
        P(),
        P(),
        P("ch", "tok", None),
        P("ch", "tok", None),
    )
    return jax.shard_map(local, mesh=mesh, in_specs=in_specs, out_specs=out_specs, check_vma=False)
```

profile of v0, /device:TPU:4, one launch (start us, length us, event | category | flops | bytes accessed | tf_op | source)
XLA Modules:
  0.0 719.0 jit_solution(10194359381156684317)
XLA Ops:
  9.2 4.7 fusion.6
  14.5 38.7 %all_to_all.63 = f32[2,64,8,256]{3,2,0,1:T(8,128)S(1)} all-to-all(f32[2,64,8,256]{3,2,0,1:T(8,128)S(1)} %copy.66), channel_id=1, replica_groups=mesh['tok'=64,'ch'=4] {'tok'}, dimensions={1} | all-to-all | bytes 2097152 | tf_op jit(solution)/shard_map/all_to_all | solution.py:19
  54.1 1.9 convolution_bitcast_fusion.5
  57.4 8.1 %all-to-all-start.1 = ((f32[128,8,256]{2,1,0:T(8,128)}), f32[128,8,256]{2,1,0:T(8,128)S(1)}, u32[]{:S(2)}, u32[]{:S(2)}) async-start(f32[128,8,256]{2,1,0:T(8,128)} %copy.68), calls=%async_computation.1 | async-start | bytes 2097152 | tf_op jit(solution)/shard_map/all_to_all | solution.py:29
  65.6 72.8 %all_gather.6 = bf16[1,256,1024]{2,0,1:T(2,128)(2,1)} all-gather(bf16[1,4,1024]{2,0,1:T(2,128)(2,1)S(1)} %copy.70), channel_id=1, replica_groups=mesh['tok'=64,'ch'=4] {'tok'}, dimensions={1}, use_global_device_ids=true | all-gather | bytes 532480 | tf_op jit(solution)/shard_map/all_gather | solution.py:38
  138.4 53.1 %all_gather.7 = bf16[1,1024,256]{2,1,0:T(8,128)(2,1)} all-gather(bf16[1,16,256]{2,1,0:T(8,128)(2,1)S(1)} %copy-done.11), channel_id=1, replica_groups=mesh['tok'=64,'ch'=4] {'tok'}, dimensions={1}, use_global_device_ids=true | all-gather | bytes 532480 | tf_op jit(solution)/shard_map/all_gather | solution.py:39
  193.1 2.4 multiply_convert_fusion
  195.4 2.2 fusion.5
  199.5 35.5 %all_to_all.64 = f32[2,64,8,256]{3,2,0,1:T(8,128)S(1)} all-to-all(f32[2,64,8,256]{3,2,0,1:T(8,128)S(1)} %copy.71), channel_id=1, replica_groups=mesh['tok'=64,'ch'=4] {'tok'}, dimensions={1} | all-to-all | bytes 2097152 | tf_op jit(solution)/shard_map/all_to_all | solution.py:19
  236.1 2.9 convolution_bitcast_fusion.4
  239.0 2.7 copy.73
  241.7 8.3 %all-to-all-start.3 = ((f32[128,8,256]{2,1,0:T(8,128)}), f32[128,8,256]{2,1,0:T(8,128)}, u32[]{:S(2)}, u32[]{:S(2)}) async-start(f32[128,8,256]{2,1,0:T(8,128)} %copy.73), calls=%async_computation.3 | async-start | bytes 2097152 | tf_op jit(solution)/shard_map/all_to_all | solution.py:29
  250.0 3.3 convolution_bitcast_fusion.1
  253.4 3.6 convolution_bitcast_fusion
  258.6 3.4 convolution_add_fusion.1
  261.9 181.6 %all-reduce.5.cloned.1.call-done = f32[1,256,1024]{2,1,0:T(8,128)} async-done(((f32[1,256,1024]{2,1,0:T(8,128)}), f32[1,256,1024]{2,1,0:T(8,128)}) %all-reduce.5.cloned.1.call-update) | async-done | bytes 1048592
  444.9 3.6 convolution_bitcast_fusion.6
  448.6 4.2 convolution_bitcast_fusion.2
  452.8 4.4 convolution_bitcast_fusion.3
  457.2 2.6 copy.76
  459.7 2.9 fusion.10
  462.7 121.8 %reduce-scatter.3.cloned.1.call-done = f32[1,16,256]{2,1,0:T(8,128)} async-done(((f32[1,1024,256]{2,1,0:T(8,128)}), f32[1,16,256]{2,1,0:T(8,128)}) %reduce-scatter.3.cloned.1.call-update) | async-done | bytes 16400 | tf_op jit(solution)/shard_map/reduce_scatter | solution.py:64
  584.5 123.4 %all-reduce.7.cloned.1.call-done = (f32[512,512]{1,0:T(8,128)}, f32[128,128]{1,0:T(8,128)}) async-done(((f32[512,512]{1,0:T(8,128)}, f32[128,128]{1,0:T(8,128)}), (f32[512,512]{1,0:T(8,128)}, f32[128,128]{1,0:T(8,128)})) %all-reduce.7.cloned.1.call-update) | async-done | bytes 1114128 | tf_op jit(solution)/shard_map/psum | solution.py:75
  707.8 2.3 copy.110
  (49 shorter events, 12.5 us)
Async XLA Ops:
  8.0 1.2 copy-start
  9.2 44.9 %copy-start.9 = (f32[128,128]{1,0:T(8,128)S(1)}, f32[128,128]{1,0:T(8,128)}, u32[]{:S(2)}) copy-start(f32[128,128]{1,0:T(8,128)} %param.10) | copy-start | bytes 196612
  14.5 51.1 %copy-start.12 = (bf16[1,4,1024]{2,1,0:T(4,128)(2,1)S(1)}, bf16[1,4,1024]{2,1,0:T(4,128)(2,1)}, u32[]{:S(2)}) copy-start(bf16[1,4,1024]{2,1,0:T(4,128)(2,1)} %param.11) | copy-start | bytes 24580
  53.1 1.0 copy-start.4
  53.1 85.3 %copy-start.11 = (bf16[1,16,256]{2,1,0:T(8,128)(2,1)S(1)}, bf16[1,16,256]{2,1,0:T(8,128)(2,1)}, u32[]{:S(2)}) copy-start(bf16[1,16,256]{2,1,0:T(8,128)(2,1)} %param.12) | copy-start | bytes 24580
  56.0 136.5 %copy-start.1 = (f32[1024,256]{1,0:T(8,128)S(1)}, f32[1024,256]{1,0:T(8,128)}, u32[]{:S(2)}) copy-start(f32[1024,256]{1,0:T(8,128)} %param.7) | copy-start | bytes 3145732
  57.4 134.0 %all-to-all-start.1 = ((f32[128,8,256]{2,1,0:T(8,128)}), f32[128,8,256]{2,1,0:T(8,128)S(1)}, u32[]{:S(2)}, u32[]{:S(2)}) async-start(f32[128,8,256]{2,1,0:T(8,128)} %copy.68), calls=%async_computation.1 | async-start | bytes 2097152 | tf_op jit(solution)/shard_map/all_to_all | solution.py:29
  191.5 1.6 copy-start.6
  191.6 1.0 copy-start.2
  193.1 2.4 copy-start.8
  193.1 2.4 copy-start.13
  197.6 1.8 copy-start.7
  235.1 1.1 copy-start.5
  241.7 206.9 %all-to-all-start.3 = ((f32[128,8,256]{2,1,0:T(8,128)}), f32[128,8,256]{2,1,0:T(8,128)}, u32[]{:S(2)}, u32[]{:S(2)}) async-start(f32[128,8,256]{2,1,0:T(8,128)} %copy.73), calls=%async_computation.3 | async-start | bytes 2097152 | tf_op jit(solution)/shard_map/all_to_all | solution.py:29
  250.0 193.6 %all-reduce.5.cloned.1.call-start = ((), (), s32[]{:S(2)}) async-start(), calls=%async_computation.6 | async-start | bytes 2097152
  253.3 4.0 copy-start.14
  253.4 331.1 %reduce-scatter.3.cloned.1.call-start = ((), (), s32[]{:S(2)}) async-start(), calls=%async_computation.5 | async-start | bytes 1064960 | tf_op jit(solution)/shard_map/reduce_scatter | solution.py:64
  257.0 450.8 %all-reduce.7.cloned.1.call-start = ((), (), s32[]{:S(2)}) async-start(), calls=%async_computation.7 | async-start | bytes 2228224 | tf_op jit(solution)/shard_map/psum | solution.py:75
  258.5 190.0 %copy-start.10 = (f32[2,512]{1,0:T(2,128)S(1)}, f32[2,512]{1,0:T(2,128)}, u32[]{:S(2)}) copy-start(f32[2,512]{1,0:T(2,128)} %param.9) | copy-start | bytes 12292
  448.6 11.2 %copy-start.3 = (f32[2,64,8,256]{3,2,1,0:T(8,128)S(1)}, f32[2,64,8,256]{3,2,1,0:T(8,128)}, u32[]{:S(2)}) copy-start(f32[2,64,8,256]{3,2,1,0:T(8,128)} %copy-done.2) | copy-start | bytes 3145732
Sparse Core Ops, SparseCore 0:
  255.2 188.3 all-reduce.4
  448.1 136.2 reduce-scatter.2
Sparse Core Ops, SparseCore 1:
  452.9 254.9 all-reduce.6
where the time goes:
time: 720 us; the launch traced here: 719 us
  waiting for transfers between devices  427 us (59%)
  blocking collectives  200 us (28%)
  matrix products  38.3 us (5%)
  local copies, waits for them, and re-layouts  17.5 us (2%)
  starting transfers between devices  16.7 us (2%)
  between operations  16.3 us (2%)
    unnamed x4, waiting for transfers between devices  182 us
    psum x1, waiting for transfers between devices, local(): grad_one, grad_two = lax.psum((one_part, two_part), ('tok', 'ch'))  123 us
    reduce_scatter x1, waiting for transfers between devices, local(): lax.psum_scatter(grad_down_part[None], 'tok', scatter_dimension=1, tiled=...  122 us
    all_to_all x2, blocking collectives, to_columns(): lax.all_to_all(block.reshape(rows, count, width // count, chans), 'tok',...  74.2 us
    all_gather x1, blocking collectives, local(): lax.all_gather(w_up, 'tok', axis=1, tiled=True)  72.8 us
    all_gather x1, blocking collectives, local(): lax.all_gather(w_down, 'tok', axis=1, tiled=True)  53.1 us
    all_to_all x2, starting transfers between devices, to_rows(): return lax.all_to_all(block, 'tok', split_axis=0, concat_axis=1, tiled=True)  16.4 us
  transfers between devices with their start and end apart: 5, of which 3 were waited for; matrix products, arithmetic and copies ran while one was open for 4% of the time, Pallas kernels for 0%

commit v1 on v0

--- a/solution.py
+++ b/solution.py
@@ -72,7 +72,7 @@
     one_part = jnp.einsum("ikc,ijc->kj", d_first, grid, precision=high)
     d_grid = jnp.einsum("kj,ikc->ijc", factor_one, d_first, precision=high)
     grad_inputs = direct + d_grid.reshape(rows * width, chans)
-    grad_one, grad_two = lax.psum((one_part, two_part), ("tok", "ch"))
+    grad_one, grad_two = lax.psum(lax.psum((one_part, two_part), "tok"), "ch")
     return (outputs, grad_inputs, grad_one, grad_two, grad_up, grad_down)
 
 

time: 720 us -> 675 us (0.938)
  waiting for transfers between devices: 427 us -> 384 us
    unnamed x4 -> x3, waiting for transfers between devices: 182 us -> 0.05 us
    psum x1 -> x2, waiting for transfers between devices: 123 us -> 236 us  [local(): grad_one, grad_two = lax.psum(lax.psum((one_part, two_part), 'tok'), 'ch')]
    all_to_all x2, waiting for transfers between devices: 0.01 us -> 20.6 us  [to_rows(): return lax.all_to_all(block, 'tok', split_axis=0, concat_axis=1, tiled=True)]
  transfers between devices with their start and end apart: 5 -> 5, of which waited for: 3 -> 4; matrix products, arithmetic and copies ran while one was open for 4% -> 4% of each run, Pallas kernels for 0% -> 0%
where the time goes in v1:
time: 675 us; the launch traced here: 674 us
  waiting for transfers between devices  384 us (57%)
  blocking collectives  200 us (30%)
  matrix products  37.1 us (5%)
  local copies, waits for them, and re-layouts  17.4 us (3%)
  starting transfers between devices  16.9 us (3%)
  between operations  14.6 us (2%)
    psum x2, waiting for transfers between devices, local(): grad_one, grad_two = lax.psum(lax.psum((one_part, two_part), 'tok'), 'ch')  236 us
    reduce_scatter x1, waiting for transfers between devices, local(): lax.psum_scatter(grad_down_part[None], 'tok', scatter_dimension=1, tiled=...  128 us
    all_to_all x2, blocking collectives, to_columns(): lax.all_to_all(block.reshape(rows, count, width // count, chans), 'tok',...  74.7 us
    all_gather x1, blocking collectives, local(): lax.all_gather(w_up, 'tok', axis=1, tiled=True)  72.8 us
    all_gather x1, blocking collectives, local(): lax.all_gather(w_down, 'tok', axis=1, tiled=True)  52.6 us
    all_to_all x2, waiting for transfers between devices, to_rows(): return lax.all_to_all(block, 'tok', split_axis=0, concat_axis=1, tiled=True)  20.6 us
    all_to_all x2, starting transfers between devices, to_rows(): return lax.all_to_all(block, 'tok', split_axis=0, concat_axis=1, tiled=True)  16.5 us
  transfers between devices with their start and end apart: 5, of which 4 were waited for; matrix products, arithmetic and copies ran while one was open for 4% of the time, Pallas kernels for 0%

profile of v1, /device:TPU:4, one launch (start us, length us, event | category | flops | bytes accessed | tf_op | source)
XLA Modules:
  0.0 673.6 jit_solution(10617461673676099044)
XLA Ops:
  8.4 4.7 fusion.6
  13.6 38.7 %all_to_all.63 = f32[2,64,8,256]{3,2,0,1:T(8,128)S(1)} all-to-all(f32[2,64,8,256]{3,2,0,1:T(8,128)S(1)} %copy.66), channel_id=1, replica_groups=mesh['tok'=64,'ch'=4] {'tok'}, dimensions={1} | all-to-all | bytes 2097152 | tf_op jit(solution)/shard_map/all_to_all | solution.py:19
  56.6 8.1 %all-to-all-start.1 = ((f32[128,8,256]{2,1,0:T(8,128)}), f32[128,8,256]{2,1,0:T(8,128)S(1)}, u32[]{:S(2)}, u32[]{:S(2)}) async-start(f32[128,8,256]{2,1,0:T(8,128)} %copy.68), calls=%async_computation.1 | async-start | bytes 2097152 | tf_op jit(solution)/shard_map/all_to_all | solution.py:29
  64.7 72.8 %all_gather.6 = bf16[1,256,1024]{2,0,1:T(2,128)(2,1)} all-gather(bf16[1,4,1024]{2,0,1:T(2,128)(2,1)S(1)} %copy.70), channel_id=1, replica_groups=mesh['tok'=64,'ch'=4] {'tok'}, dimensions={1}, use_global_device_ids=true | all-gather | bytes 532480 | tf_op jit(solution)/shard_map/all_gather | solution.py:38
  137.5 52.6 %all_gather.7 = bf16[1,1024,256]{2,1,0:T(8,128)(2,1)} all-gather(bf16[1,16,256]{2,1,0:T(8,128)(2,1)S(1)} %copy-done.13), channel_id=1, replica_groups=mesh['tok'=64,'ch'=4] {'tok'}, dimensions={1}, use_global_device_ids=true | all-gather | bytes 532480 | tf_op jit(solution)/shard_map/all_gather | solution.py:39
  191.8 2.4 multiply_convert_fusion
  194.1 2.2 fusion.5
  198.2 36.0 %all_to_all.64 = f32[2,64,8,256]{3,2,0,1:T(8,128)S(1)} all-to-all(f32[2,64,8,256]{3,2,0,1:T(8,128)S(1)} %copy.71), channel_id=1, replica_groups=mesh['tok'=64,'ch'=4] {'tok'}, dimensions={1} | all-to-all | bytes 2097152 | tf_op jit(solution)/shard_map/all_to_all | solution.py:19
  235.3 2.9 convolution_bitcast_fusion.4
  238.2 2.6 copy.73
  240.8 8.4 %all-to-all-start.3 = ((f32[128,8,256]{2,1,0:T(8,128)}), f32[128,8,256]{2,1,0:T(8,128)}, u32[]{:S(2)}, u32[]{:S(2)}) async-start(f32[128,8,256]{2,1,0:T(8,128)} %copy.73), calls=%async_computation.3 | async-start | bytes 2097152 | tf_op jit(solution)/shard_map/all_to_all | solution.py:29
  249.5 3.5 convolution_bitcast_fusion.1
  253.1 2.1 convolution_bitcast_fusion.6
  255.2 20.6 %all-to-all-done.3 = f32[128,8,256]{2,1,0:T(8,128)} async-done(((f32[128,8,256]{2,1,0:T(8,128)}), f32[128,8,256]{2,1,0:T(8,128)}, u32[]{:S(2)}, u32[]{:S(2)}) %all-to-all-start.3) | async-done | bytes 1048608 | tf_op jit(solution)/shard_map/all_to_all | solution.py:29
  275.8 4.1 convolution_bitcast_fusion.2
  280.0 3.7 convolution_bitcast_fusion
  285.0 183.1 %all-reduce.6.cloned.1.call-done = (f32[512,512]{1,0:T(8,128)}, f32[128,128]{1,0:T(8,128)}, f32[1,256,1024]{2,1,0:T(8,128)}) async-done(((f32[512,512]{1,0:T(8,128)}, f32[128,128]{1,0:T(8,128)}, f32[1,256,1024]{2,1,0:T(8,128)}), (f32[512,512]{1,0:T(8,128)}, f32[128,128]{1,0:T(8,128)}, f32[1,256,1024]{2,1,0:T(8,128)})) %all-reduce.6.cloned.1.call-update) | async-done | bytes 2162704 | tf_op jit(solution)/shard_map/psum | solution.py:75
  468.1 3.4 convolution_add_fusion.1
  471.5 4.5 convolution_bitcast_fusion.3
  475.9 2.5 copy.76
  478.5 2.9 fusion.10
  482.8 127.5 %reduce-scatter.3.cloned.1.call-done = f32[1,16,256]{2,1,0:T(8,128)} async-done(((f32[1,1024,256]{2,1,0:T(8,128)}), f32[1,16,256]{2,1,0:T(8,128)}) %reduce-scatter.3.cloned.1.call-update) | async-done | bytes 16400 | tf_op jit(solution)/shard_map/reduce_scatter | solution.py:64
  610.3 53.1 %all-reduce.8.cloned.1.call-done = (f32[512,512]{1,0:T(8,128)}, f32[128,128]{1,0:T(8,128)}) async-done(((f32[512,512]{1,0:T(8,128)}, f32[128,128]{1,0:T(8,128)}), (f32[512,512]{1,0:T(8,128)}, f32[128,128]{1,0:T(8,128)})) %all-reduce.8.cloned.1.call-update) | async-done | bytes 1114128 | tf_op jit(solution)/shard_map/psum | solution.py:75
  663.4 2.3 copy.112
  (53 shorter events, 14.4 us)
Async XLA Ops:
  7.2 1.2 copy-start
  8.4 44.9 %copy-start.11 = (f32[128,128]{1,0:T(8,128)S(1)}, f32[128,128]{1,0:T(8,128)}, u32[]{:S(2)}) copy-start(f32[128,128]{1,0:T(8,128)} %param.10) | copy-start | bytes 196612
  13.6 51.1 %copy-start.14 = (bf16[1,4,1024]{2,1,0:T(4,128)(2,1)S(1)}, bf16[1,4,1024]{2,1,0:T(4,128)(2,1)}, u32[]{:S(2)}) copy-start(bf16[1,4,1024]{2,1,0:T(4,128)(2,1)} %param.11) | copy-start | bytes 24580
  52.3 1.0 copy-start.4
  52.3 85.2 %copy-start.13 = (bf16[1,16,256]{2,1,0:T(8,128)(2,1)S(1)}, bf16[1,16,256]{2,1,0:T(8,128)(2,1)}, u32[]{:S(2)}) copy-start(bf16[1,16,256]{2,1,0:T(8,128)(2,1)} %param.12) | copy-start | bytes 24580
  55.2 136.1 %copy-start.1 = (f32[1024,256]{1,0:T(8,128)S(1)}, f32[1024,256]{1,0:T(8,128)}, u32[]{:S(2)}) copy-start(f32[1024,256]{1,0:T(8,128)} %param.7) | copy-start | bytes 3145732
  56.6 133.6 %all-to-all-start.1 = ((f32[128,8,256]{2,1,0:T(8,128)}), f32[128,8,256]{2,1,0:T(8,128)S(1)}, u32[]{:S(2)}, u32[]{:S(2)}) async-start(f32[128,8,256]{2,1,0:T(8,128)} %copy.68), calls=%async_computation.1 | async-start | bytes 2097152 | tf_op jit(solution)/shard_map/all_to_all | solution.py:29
  190.2 1.6 copy-start.8
  190.2 1.0 copy-start.2
  191.8 2.4 copy-start.10
  191.8 2.4 copy-start.15
  196.3 1.8 copy-start.9
  234.3 1.1 copy-start.6
  240.8 35.0 %copy-start.12 = (f32[2,512]{1,0:T(2,128)S(1)}, f32[2,512]{1,0:T(2,128)}, u32[]{:S(2)}) copy-start(f32[2,512]{1,0:T(2,128)} %param.9) | copy-start | bytes 12292
  240.8 35.0 %all-to-all-start.3 = ((f32[128,8,256]{2,1,0:T(8,128)}), f32[128,8,256]{2,1,0:T(8,128)}, u32[]{:S(2)}, u32[]{:S(2)}) async-start(f32[128,8,256]{2,1,0:T(8,128)} %copy.73), calls=%async_computation.3 | async-start | bytes 2097152 | tf_op jit(solution)/shard_map/all_to_all | solution.py:29
  249.3 218.8 %all-reduce.6.cloned.1.call-start = ((), (), s32[]{:S(2)}) async-start(), calls=%async_computation.6 | async-start | bytes 4325376 | tf_op jit(solution)/shard_map/psum | solution.py:75
  249.5 3.6 copy-start.5
  249.5 3.6 copy-start.7
  279.9 3.8 copy-start.16
  280.0 330.3 %reduce-scatter.3.cloned.1.call-start = ((), (), s32[]{:S(2)}) async-start(), calls=%async_computation.5 | async-start | bytes 1064960 | tf_op jit(solution)/shard_map/reduce_scatter | solution.py:64
  283.7 379.7 %all-reduce.8.cloned.1.call-start = ((), (), s32[]{:S(2)}) async-start(), calls=%async_computation.7 | async-start | bytes 2228224 | tf_op jit(solution)/shard_map/psum | solution.py:75
  471.5 7.0 %copy-start.3 = (f32[2,64,8,256]{3,2,1,0:T(8,128)S(1)}, f32[2,64,8,256]{3,2,1,0:T(8,128)}, u32[]{:S(2)}) copy-start(f32[2,64,8,256]{3,2,1,0:T(8,128)} %copy-done.2) | copy-start | bytes 3145732
Sparse Core Ops, SparseCore 0:
  280.1 187.9 all-reduce.5
  472.7 137.6 reduce-scatter.2
  612.8 50.5 all-reduce.7
